TPU v7x, 512 devices: a whole 4x8x8 slice. The times are simulated.
512 devices in a mesh: ctx: 64 (over z, y_hi, x), tp: 8 (over y_lo, core).
Axes of the slice: x: 4, y: 8 (y_hi: 2, y_lo: 4; y = y_hi * 4 + y_lo), z: 8, core: 2. Of those that a mesh axis runs over, the one named last changes fastest.
Arguments:
- tokens: bfloat16 [8192, 4096], P('ctx'), may hold values from -6 to 6
- weights: bfloat16 [8, 512, 3, 4096], P('tp', 'ctx'), may hold values from -0.09375 to 0.09375
- residues: float32 [8, 512, 16], P('tp', 'ctx'), may hold values from -1.5 to 1.5
- decay_rates: float32 [8, 512, 16], P('tp', 'ctx'), may hold values from 6.1035156e-05 to 0.03
- cotangent: bfloat16 [4096, 8192], P('tp', 'ctx'), may hold values from -6 to 6
Outputs:
- hyena_out: bfloat16 [4096, 8192], P('tp', 'ctx')
- grad_input: bfloat16 [8192, 4096], P('ctx', 'tp')
- grad_residue: float32 [8, 512, 16], P('tp', 'ctx')
All inputs are finite; a program needn't handle non-finite values.
Results may differ from a plain program's by a relative error of at most 0.018.
Values may be sent and summed in bfloat16 or wider, within the bound.
A program may use at most 64 MiB of HBM per device.

v0:
```python
import functools
import math

import jax
import jax.numpy as jnp
from jax import lax
from jax.experimental import pallas as pl
from jax.experimental.pallas import tpu as pltpu
from jax.sharding import Mesh, PartitionSpec as P

AXES = ("z", "h", "x", "l", "c")
SIZES = (8, 2, 4, 4, 2)
Z, H, X, NL, NC = SIZES
ZH = Z * H
MESH = pl.DeviceIdType.MESH
F32 = jnp.float32
BF16 = jnp.bfloat16

D = 4096
POS = 128
OWN = 8
CH = ZH * OWN
ROWS = X * POS
M = 16
SUB = 64
COLS = D // (NL * NC)
HALF = COLS // 2
UNIT = POS // 4
ORDER = (0, 3, 1, 2)
STEPS = ((Z // 2, Z - 1 - Z // 2), (Z - 1 - Z // 2, Z // 2))


def remote(src, dst, send, recv, device):
    return pltpu.make_async_remote_copy(
        src_ref=src, dst_ref=dst, send_sem=send, recv_sem=recv,
        device_id=device, device_id_type=MESH,
    )


def rounded(value):
    return value.astype(BF16).astype(F32)


def tree_sum(terms):
    terms = list(terms)
    while len(terms) > 1:
        terms = [
            terms[i] + terms[i + 1] if i + 1 < len(terms) else terms[i]
            for i in range(0, len(terms), 2)
        ]
    return terms[0]


def rows_of(index, count):
    return pl.ds(pl.multiple_of(index * count, count), count)


def body(
    length,
    tok, wts, res, rate, cot,
    hyena_out, grad_input, grad_residue,
    tk, wg, coef_own, coef, cotv,
    q_s, k_s, v_s, g_s, s_s, cot_s, conv_s, back_s,
    a_t, r_t, cl_t, cb_t, eb, pb, st, gr_s, gr_t, gr_r,
    hy_t, hy_o, g_mat, acc, d_s, d_r, m1_s, m1_r, m2_s, m2_r, y_s, y_r, y_own,
    loc_sem, w_ss, w_rs, c_ss, c_rs, h_ss, h_rs, t_ss, t_rs, p_ss, p_rs,
    ct_ss, ct_rs, pb_ss, pb_rs, st_ss, st_rs, gr_ss, gr_rs, hy_ss, hy_rs,
    d_ss, d_rs, m1_ss, m1_rs, m2_ss, m2_rs, y_ss, y_rs,
):
    z, h, x = lax.axis_index("z"), lax.axis_index("h"), lax.axis_index("x")
    ell, core = lax.axis_index("l"), lax.axis_index("c")
    me = z * H + h
    z_up, z_down = lax.rem(z + 1, Z), lax.rem(z + Z - 1, Z)
    x_up, x_down, x_far = lax.rem(x + 1, X), lax.rem(x + X - 1, X), lax.rem(x + 2, X)
    mate = me + 1 - 2 * h
    sends = []

    coef_own[...] = jnp.zeros_like(coef_own)
    coef_own[0, :, 0:M] = res[0]
    coef_own[1, :, 0:M] = rate[0]
    local = [
        pltpu.make_async_copy(tok, tk.at[rows_of(x, POS), :], loc_sem.at[0]),
        pltpu.make_async_copy(wts, wg.at[:, rows_of(me, OWN), :], loc_sem.at[1]),
        pltpu.make_async_copy(cot.at[:, x], cotv.at[x], loc_sem.at[2]),
    ]
    for copy in local:
        copy.start()
    coef[:, rows_of(me, OWN), :] = coef_own[...]

    barrier = pltpu.get_barrier_semaphore()
    peers = [{"z": z_up}, {"z": z_down}, {"h": 1 - h}, {"c": 1 - core}]
    peers += [{"x": lax.rem(x + i, X)} for i in range(1, X)]
    peers += [{"l": lax.rem(ell + i, NL)} for i in range(1, NL)]
    for peer in peers:
        pl.semaphore_signal(barrier, inc=1, device_id=peer, device_id_type=MESH)
    pl.semaphore_wait(barrier, len(peers))

    def ring(stream, way, step):
        from_z = lax.rem(z - step + Z, Z) if way == 0 else lax.rem(z + step, Z)
        block = from_z * H + (h if stream == 0 else 1 - h)
        slot = wg.at[:, rows_of(block, OWN), :]
        cslot = coef.at[:, rows_of(block, OWN), :]
        own = stream == 0 and step == 0
        to = {"z": z_up if way == 0 else z_down}
        return (
            remote(wts if own else slot, slot, w_ss.at[stream, way, step], w_rs.at[stream, way, step], to),
            remote(coef_own if own else cslot, cslot, c_ss.at[stream, way, step], c_rs.at[stream, way, step], to),
        )

    def launch(copies):
        for copy in copies:
            copy.start()
            sends.append(copy)
        return copies

    def arrived(copies):
        for copy in copies:
            copy.wait_recv()

    def unit(source, u):
        return tk.at[pl.ds(pl.multiple_of(source * POS + core * (POS // 2) + u * UNIT, UNIT), UNIT), :]

    def own_unit(u):
        return tok.at[pl.ds(pl.multiple_of(core * (POS // 2) + u * UNIT, UNIT), UNIT), :]

    def tok_own(way, u):
        to = {"x": x_up if way == 0 else x_down}
        return remote(own_unit(u), unit(x, u), t_ss.at[way, u], t_rs.at[way, u], to)

    def tok_far(way):
        to = {"x": x_up if way == 0 else x_down}
        src = unit(x_down if way == 0 else x_up, way)
        return remote(src, src, t_ss.at[way, 2], t_rs.at[way, 2], to)

    def pass_on(index, source, u):
        src = unit(source, u)
        return remote(src, src, p_ss.at[index], p_rs.at[index], {"c": 1 - core})

    mate_slot = wg.at[:, rows_of(me, OWN), :]
    to_mate = launch((
        remote(wts, mate_slot, h_ss.at[0], h_rs.at[0], {"h": 1 - h}),
        remote(coef_own, coef.at[:, rows_of(me, OWN), :], h_ss.at[1], h_rs.at[1], {"h": 1 - h}),
    ))
    flying = {}
    for way in (0, 1):
        flying[0, way] = launch(ring(0, way, 0))
    toks = {}
    for way, u in ((0, 0), (1, 1), (0, 1), (1, 0)):
        toks[way, u] = launch((tok_own(way, u),))
    cots = [
        remote(cot.at[:, lax.rem(x + i, X)], cotv.at[x], ct_ss.at[i - 1], ct_rs.at[i - 1], {"x": lax.rem(x + i, X)})
        for i in range(1, X)
    ]
    launch(cots)

    def advance(stream, step):
        for way in (0, 1):
            if step < STEPS[stream][way]:
                arrived(flying[stream, way])
                if step + 1 < STEPS[stream][way]:
                    flying[stream, way] = launch(ring(stream, way, step + 1))

    passes = []
    arrived(toks[0, 0])
    far_up = launch((tok_far(0),))
    passes += launch((pass_on(0, x_down, 0),))
    arrived(toks[1, 1])
    far_down = launch((tok_far(1),))
    passes += launch((pass_on(1, x_up, 1),))
    advance(0, 0)
    arrived(to_mate)
    for way in (0, 1):
        flying[1, way] = launch(ring(1, way, 0))
    arrived(toks[0, 1])
    passes += launch((pass_on(2, x_down, 1),))
    arrived(toks[1, 0])
    passes += launch((pass_on(3, x_up, 0),))
    advance(0, 1)
    advance(1, 0)
    arrived(far_up)
    passes += launch((pass_on(4, x_far, 0),))
    arrived(far_down)
    passes += launch((pass_on(5, x_far, 1),))
    advance(0, 2)
    advance(1, 1)
    arrived(cots)
    advance(0, 3)
    advance(1, 2)
    arrived(passes)
    advance(1, 3)
    for copy in local:
        copy.wait()

    def project(i, carry):
        out = lax.dot_general(
            tk[rows_of(i, POS), :], wg[...].reshape(3 * CH, D),
            (((1,), (1,)), ((), ())), preferred_element_type=F32,
        )
        q_s[rows_of(i, POS), :] = rounded(out[:, 0:CH])
        k_s[rows_of(i, POS), :] = rounded(out[:, CH:2 * CH])
        v_s[rows_of(i, POS), :] = rounded(out[:, 2 * CH:3 * CH])
        return carry

    lax.fori_loop(0, X, project, 0)

    def gate(i, carry):
        at = rows_of(i, POS)
        cot_s[at, :] = jnp.transpose(cotv[i].astype(F32).reshape(CH, POS))
        g_s[at, :] = rounded(k_s[at, :] * v_s[at, :])
        s_s[at, :] = rounded(cot_s[at, :] * q_s[at, :])
        return carry

    lax.fori_loop(0, X, gate, 0)

    residue = jnp.transpose(coef[0])[0:M, :]
    decay = jnp.transpose(coef[1])[0:M, :]
    width = jnp.sqrt(2.0 * decay)
    once = jnp.exp(-decay)
    scaled = residue * width
    for m in range(M):
        a_t[m] = jnp.broadcast_to(once[m:m + 1, :], (8, CH))
        r_t[m] = jnp.broadcast_to(scaled[m:m + 1, :], (8, CH))

    def states(t, carry):
        up, down = carry
        g_now = g_s[pl.ds(t, 8, stride=SUB), :]
        s_now = s_s[pl.ds(SUB - 1 - t, 8, stride=SUB), :]
        return (
            tuple(a_t[m] * up[m] + g_now for m in range(M)),
            tuple(a_t[m] * down[m] + s_now for m in range(M)),
        )

    zero = tuple(jnp.zeros((8, CH), F32) for _ in range(M))
    up, down = lax.fori_loop(0, SUB, states, (zero, zero))
    piece = lax.broadcasted_iota(jnp.int32, (8, CH), 0)
    for m in range(M):
        lost = decay[m:m + 1, :]
        fore, aft = up[m], down[m]
        for shift in (1, 2, 4):
            keep = jnp.exp(lost * (-float(SUB * shift)))
            fore = fore + jnp.where(piece >= shift, keep * pltpu.roll(fore, shift, 0), 0.0)
            aft = aft + jnp.where(piece < 8 - shift, keep * pltpu.roll(aft, 8 - shift, 0), 0.0)
        eb[0, m:m + 1, :] = fore[7:8, :]
        eb[1, m:m + 1, :] = aft[0:1, :]
        cl_t[m] = jnp.where(piece >= 1, pltpu.roll(fore, 1, 0), 0.0)
        cb_t[m] = jnp.where(piece < 7, pltpu.roll(aft, 7, 0), 0.0)

    to_pair = launch((remote(eb, pb, pb_ss, pb_rs, {"h": 1 - h}),))
    direct = []
    for i in range(1, Z):
        to_z = lax.rem(z + i, Z)
        which = jnp.where(to_z > z, 0, 1)
        direct.append(remote(eb.at[which], st.at[me], st_ss.at[0, i], st_rs.at[0, i], {"z": to_z}))
    launch(direct)
    arrived(to_pair)
    relayed = []
    for i in range(1, Z):
        to_z = lax.rem(z + i, Z)
        which = jnp.where(to_z > z, 0, 1)
        relayed.append(remote(pb.at[which], st.at[mate], st_ss.at[1, i], st_rs.at[1, i], {"z": to_z}))
    launch(relayed)
    st[mate] = pb[1 - h]
    arrived(direct)
    arrived(relayed)

    far_keep = jnp.exp(decay * (-float(ROWS)))
    none = jnp.zeros((M, CH), F32)
    before = lax.fori_loop(0, me, lambda j, s: far_keep * s + st[j], none)
    after = lax.fori_loop(0, ZH - 1 - me, lambda j, s: far_keep * s + st[ZH - 1 - j], none)

    place = piece.astype(F32) * float(SUB)
    start_up, start_down = [], []
    for m in range(M):
        lost = decay[m:m + 1, :]
        start_up.append(cl_t[m] + jnp.exp(-lost * place) * before[m:m + 1, :])
        start_down.append(
            cb_t[m] + jnp.exp(-lost * (float(SUB * 7) - place)) * after[m:m + 1, :]
        )

    def forward(t, carry):
        up, total = carry
        at = pl.ds(t, 8, stride=SUB)
        g_now, s_now = g_s[at, :], s_s[at, :]
        up = tuple(a_t[m] * up[m] + g_now for m in range(M))
        conv_s[at, :] = tree_sum(r_t[m] * up[m] for m in range(M))
        return up, tuple(total[m] + s_now * up[m] for m in range(M))

    def backward(t, down):
        at = pl.ds(SUB - 1 - t, 8, stride=SUB)
        s_now = s_s[at, :]
        down = tuple(a_t[m] * down[m] + s_now for m in range(M))
        back_s[at, :] = tree_sum(r_t[m] * down[m] for m in range(M))
        return down

    _, total = lax.fori_loop(0, SUB, forward, (tuple(start_up), zero))
    lax.fori_loop(0, SUB, backward, tuple(start_down))

    def gates(i, carry):
        at = rows_of(i, POS)
        conv, back = rounded(conv_s[at, :]), rounded(back_s[at, :])
        g_mat[at, 0:CH] = (cot_s[at, :] * conv).astype(BF16)
        g_mat[at, CH:2 * CH] = (back * v_s[at, :]).astype(BF16)
        g_mat[at, 2 * CH:3 * CH] = (back * k_s[at, :]).astype(BF16)
        hyena = jnp.transpose(q_s[at, :] * conv)
        hy_t[i] = hyena.reshape(ZH, OWN, POS).astype(BF16)
        return carry

    lax.fori_loop(0, X, gates, 0)
    hyenas = [
        remote(hy_t.at[lax.rem(x + i, X)], hy_o.at[:, x], hy_ss.at[i - 1], hy_rs.at[i - 1], {"x": lax.rem(x + i, X)})
        for i in range(1, X)
    ]
    launch(hyenas)
    hy_o[:, x] = hy_t[x]

    gr_s[...] = jnp.zeros_like(gr_s)
    norm = 1.0 / math.sqrt(length)
    for m in range(M):
        gr_s[m:m + 1, :] = jnp.sum(total[m], axis=0, keepdims=True) * (width[m:m + 1, :] * norm)
    gr_t[...] = jnp.transpose(gr_s[...])
    owners = []
    for i in range(1, ZH):
        to = lax.rem(me + i, ZH)
        owners.append(remote(
            gr_t.at[rows_of(to, OWN), :], gr_r.at[i], gr_ss.at[i], gr_rs.at[i],
            {"z": lax.div(to, H), "h": lax.rem(to, H)},
        ))
    launch(owners)

    def product(j, mine):
        parity = core if mine else 1 - core
        col = pl.multiple_of((j * NC + parity) * COLS, COLS)

        def tile(i, carry):
            at = rows_of(i, 2 * POS)
            out = jnp.dot(
                g_mat[at, :], wg[:, :, pl.ds(col, COLS)].reshape(3 * CH, COLS),
                preferred_element_type=F32,
            )
            if mine:
                acc[j, at, :] = out
            else:
                d_s[j, at, :] = out.astype(BF16)
            return carry

        lax.fori_loop(0, ROWS // (2 * POS), tile, 0)

    def chip_sum(j, owner):
        at = rows_of(owner, POS)
        return acc[j, at, :] + d_r[j, at, :].astype(F32)

    cores, first, second, finals = {}, {}, {}, {}
    for j in ORDER:
        product(j, False)
        cores[j] = launch((remote(d_s.at[j], d_r.at[j], d_ss.at[j], d_rs.at[j], {"c": 1 - core}),))
        product(j, True)

    def stage_first(j):
        arrived(cores[j])
        far = chip_sum(j, x_far)
        m1_s[j, 0] = far[:, 0:HALF].astype(BF16)
        m1_s[j, 1] = far[:, HALF:COLS].astype(BF16)
        first[j] = launch([
            remote(m1_s.at[j, w], m1_r.at[j, w], m1_ss.at[j, w], m1_rs.at[j, w], {"x": x_up if w == 0 else x_down})
            for w in (0, 1)
        ])

    def stage_second(j):
        arrived(first[j])
        for w in (0, 1):
            near = chip_sum(j, x_up if w == 0 else x_down)
            cut = slice(0, HALF) if w == 0 else slice(HALF, COLS)
            rest = slice(HALF, COLS) if w == 0 else slice(0, HALF)
            m2_s[j, w, :, cut] = (near[:, cut] + m1_r[j, w].astype(F32)).astype(BF16)
            m2_s[j, w, :, rest] = near[:, rest].astype(BF16)
        second[j] = launch([
            remote(m2_s.at[j, w], m2_r.at[j, w], m2_ss.at[j, w], m2_rs.at[j, w], {"x": x_up if w == 0 else x_down})
            for w in (0, 1)
        ])

    def stage_third(j):
        arrived(second[j])
        total_x = chip_sum(j, x) + m2_r[j, 0].astype(F32) + m2_r[j, 1].astype(F32)
        copy = remote(y_s.at[j], y_r.at[ell], y_ss.at[j], y_rs.at[ell], {"l": jnp.int32(j)})
        finals[j] = copy

        @pl.when(ell == j)
        def _():
            y_own[...] = total_x

        @pl.when(ell != j)
        def _():
            y_s[j] = total_x.astype(BF16)
            copy.start()

    first_of, n = ORDER, len(ORDER)
    for i in range(n + 2):
        if i < n:
            stage_first(first_of[i])
        if 0 <= i - 1 < n:
            stage_second(first_of[i - 1])
        if 0 <= i - 2 < n:
            stage_third(first_of[i - 2])

    arrived(hyenas)
    hyena_out[...] = hy_o[...]
    arrived(owners)
    share = gr_t[rows_of(me, OWN), :]
    for i in range(1, ZH):
        share = share + gr_r[i]
    grad_residue[...] = share[:, 0:M]
    for j in range(NL):
        @pl.when(ell != j)
        def _():
            remote(y_s.at[j], y_r.at[j], y_ss.at[j], y_rs.at[j], {"l": jnp.int32(j)}).wait_recv()
            y_own[...] += y_r[j].astype(F32)
            finals[j].wait_send()
    grad_input[...] = y_own[...].astype(BF16)
    for copy in sends:
        copy.wait_send()


def shards(tokens, weights, residues, decay_rates, cotangent, length):
    wts = jnp.transpose(weights[0], (1, 0, 2))
    cot = cotangent.reshape(ZH, X, OWN, POS)
    dma = pltpu.SemaphoreType.DMA
    scratch = [
        pltpu.VMEM((ROWS, D), BF16),
        pltpu.VMEM((3, CH, D), BF16),
        pltpu.VMEM((2, OWN, 128), F32),
        pltpu.VMEM((2, CH, 128), F32),
        pltpu.VMEM((X, ZH, OWN, POS), BF16),
    ]
    scratch += [pltpu.VMEM((ROWS, CH), F32)] * 8
    scratch += [pltpu.VMEM((M, 8, CH), F32)] * 4
    scratch += [
        pltpu.VMEM((2, M, CH), F32),
        pltpu.VMEM((2, M, CH), F32),
        pltpu.VMEM((ZH, M, CH), F32),
        pltpu.VMEM((CH, CH), F32),
        pltpu.VMEM((CH, CH), F32),
        pltpu.VMEM((ZH, OWN, CH), F32),
        pltpu.VMEM((X, ZH, OWN, POS), BF16),
        pltpu.VMEM((ZH, X, OWN, POS), BF16),
        pltpu.VMEM((ROWS, 3 * CH), BF16),
        pltpu.VMEM((NL, ROWS, COLS), F32),
        pltpu.VMEM((NL, ROWS, COLS), BF16),
        pltpu.VMEM((NL, ROWS, COLS), BF16),
        pltpu.VMEM((NL, 2, POS, HALF), BF16),
        pltpu.VMEM((NL, 2, POS, HALF), BF16),
        pltpu.VMEM((NL, 2, POS, COLS), BF16),
        pltpu.VMEM((NL, 2, POS, COLS), BF16),
        pltpu.VMEM((NL, POS, COLS), BF16),
        pltpu.VMEM((NL, POS, COLS), BF16),
        pltpu.VMEM((POS, COLS), F32),
    ]
    steps = Z // 2
    scratch += [dma((3,))]
    for shape in (
        (2, 2, steps), (2, 2, steps), (2,), (2, 3), (6,), (X - 1,), (), (2, Z), (ZH,), (X - 1,),
        (NL,), (NL, 2), (NL, 2), (NL,),
    ):
        scratch += [dma(shape) if shape else dma, dma(shape) if shape else dma]
    vmem, hbm = pl.BlockSpec(memory_space=pltpu.VMEM), pl.BlockSpec(memory_space=pl.ANY)
    hyena, grad, residue = pl.pallas_call(
        functools.partial(body, length),
        out_shape=(
            jax.ShapeDtypeStruct((ZH, X, OWN, POS), BF16),
            jax.ShapeDtypeStruct((POS, COLS), BF16),
            jax.ShapeDtypeStruct((OWN, M), F32),
        ),
        in_specs=[hbm, hbm, vmem, vmem, hbm],
        out_specs=(vmem, vmem, vmem),
        scratch_shapes=scratch,
        compiler_params=pltpu.CompilerParams(
            collective_id=0, has_side_effects=True, vmem_limit_bytes=60 * 1024 * 1024
        ),
        name="hyena_block",
    )(tokens, wts, residues, decay_rates, cot)
    return (hyena.reshape(X * ZH * OWN, POS), grad, residue[None])


def solution(mesh):
    fine = Mesh(mesh.devices.reshape(SIZES), AXES)
    ctx, tp = ("z", "h", "x"), ("l", "c")

    def step(tokens, weights, residues, decay_rates, cotangent):
        return jax.shard_map(
            functools.partial(shards, length=tokens.shape[0]),
            mesh=fine,
            in_specs=(P(ctx, None), P(tp, ctx), P(tp, ctx), P(tp, ctx), P(tp, ctx)),
            out_specs=(P(tp, ctx), P(ctx, tp), P(tp, ctx)),
            check_vma=False,
        )(tokens, weights, residues, decay_rates, cotangent)

    return step
```

profile of v0, /device:TPU:16, one launch (start us, length us, event | category | flops | bytes accessed | tf_op | source)
XLA Modules:
  0.0 111.6 jit_solution(823245727523665829)
XLA Ops:
  0.6 108.1 %hyena_block.1 = (bf16[16,4,8,128]{3,2,1,0:T(8,128)(2,1)}, bf16[128,512]{1,0:T(8,128)(2,1)}, f32[8,16]{1,0:T(8,128)}) custom-call(bf16[128,4096]{1,0:T(8,128)(2,1)} %tok.1, bf16[3,8,4096]{2,1,0:T(8,128)(2,1)} %bitcast.6, f32[1,8,16]{2,1,0:T(8,128)} %res.1, f32[1,8,16]{2,1,0:T(8,128)} %rate.1, bf16[16,4,8,128]{3,2,1,0:T(8,128)(2,1)} %bitcast.8), custom_call_target="tpu_custom_call" | custom-call | tf_op jit(solution)/shard_map/hyena_block/pallas_call | solution.py:465
  108.7 0.0 copy-start
  108.7 1.6 %copy.11 = bf16[512,128]{1,0:T(8,128)(2,1)} copy(bf16[512,128]{1,0:T(8,128)(2,1)} %bitcast.7) | data formatting | bytes 262144
  110.3 0.0 copy-done
  110.3 0.0 copy-start.1
  110.4 0.7 copy.12
  111.0 0.0 copy-done.1
  111.0 0.6 copy.13
Async XLA Ops:
  108.7 1.6 %copy-start = (bf16[128,512]{1,0:T(8,128)(2,1)S(1)}, bf16[128,512]{1,0:T(8,128)(2,1)}, u32[]{:S(2)}) copy-start(bf16[128,512]{1,0:T(8,128)(2,1)} %get-tuple-element.13) | copy-start | bytes 393220
  110.3 0.7 copy-start.1
where the time goes:
time: 112 us
  Pallas kernels  108 us (96%)
  local copies, waits for them, and re-layouts  2.88 us (3%)
    pallas_call x1, Pallas kernels, shards(): pl.pallas_call(functools.partial(body, length), out_shape=(jax.ShapeDtype...  108 us
    unnamed x7, local copies, waits for them, and re-layouts  2.88 us

commit v1 on v0

v1 whole, which is shorter than its diff:
```python
import functools
import heapq
import math

import jax
import jax.numpy as jnp
from jax import lax
from jax.experimental import pallas as pl
from jax.experimental.pallas import tpu as pltpu
from jax.sharding import Mesh, PartitionSpec as P

AXES = ("z", "h", "x", "l", "c")
SIZES = (8, 2, 4, 4, 2)
Z, H, X, NL, NC = SIZES
ZH = Z * H
MESH = pl.DeviceIdType.MESH
F32 = jnp.float32
BF16 = jnp.bfloat16

D = 4096
POS = 128
OWN = 8
CH = ZH * OWN
ROWS = X * POS
M = 16
SUB = 64
COLS = D // (NL * NC)
PARTS = 2
WIDE = COLS // PARTS
HALF = WIDE // 2
PIECES = NL * PARTS
UNIT = POS // 4
CUT = D // 2
CHUNKS = 6
ORDER = (0, 6, 1, 7, 2, 4, 3, 5)
STEPS = ((Z // 2, Z - 1 - Z // 2), (Z - 1 - Z // 2, Z // 2))


def arrival_order():
    cost = {"z": 0.7, "h": 1.4, "x": 5.6, "c": 0.8}
    delay = {"z": 3.5, "h": 5.0, "x": 2.5, "c": 1.5}
    free, queue, order = {}, [], []

    def send(now, link, message):
        free[link] = max(now, free.get(link, 0.0)) + cost[link[0]]
        heapq.heappush(queue, (free[link] + delay[link[0]], len(order) + len(queue), message))

    for p in range(CHUNKS):
        for way in (0, 1):
            send(0.0, ("z", way), ("ring", 0, way, 0, p))
        send(0.0, ("h",), ("mate", p))
    for way in (0, 1):
        for u in (way, 1 - way):
            send(0.0, ("x", way), ("near", way, u))
    while queue:
        now, _, message = heapq.heappop(queue)
        order.append(message)
        if message[0] == "ring":
            _, stream, way, step, p = message
            if step + 1 < STEPS[stream][way]:
                send(now, ("z", way), ("ring", stream, way, step + 1, p))
        elif message[0] == "mate":
            for way in (0, 1):
                send(now, ("z", way), ("ring", 1, way, 0, message[1]))
        elif message[0] == "near":
            _, way, u = message
            if u == way:
                send(now, ("x", way), ("far", way))
            send(now, ("c",), ("pass", 2 * way + u))
        elif message[0] == "far":
            send(now, ("c",), ("pass", 4 + message[1]))
    return order


def remote(src, dst, send, recv, device):
    return pltpu.make_async_remote_copy(
        src_ref=src, dst_ref=dst, send_sem=send, recv_sem=recv,
        device_id=device, device_id_type=MESH,
    )


def rounded(value):
    return value.astype(BF16).astype(F32)


def tree_sum(terms):
    terms = list(terms)
    while len(terms) > 1:
        terms = [
            terms[i] + terms[i + 1] if i + 1 < len(terms) else terms[i]
            for i in range(0, len(terms), 2)
        ]
    return terms[0]


def rows_of(index, count):
    return pl.ds(pl.multiple_of(index * count, count), count)


def body(
    length,
    tok, wts, res, rate, cot,
    hyena_out, grad_input, grad_residue,
    tk, wg, coef_own, coef, cotv,
    q_s, k_s, v_s, g_s, s_s, cot_s, conv_s, back_s,
    a_t, r_t, cl_t, cb_t, eb, st, gr_s, gr_t, gr_r,
    hy_t, hy_o, g_mat, acc, d_s, d_r, m1_s, m1_r, m2_s, m2_r, y_s, y_r, y_own,
    loc_sem, w_ss, w_rs, c_ss, c_rs, h_ss, h_rs, t_ss, t_rs, p_ss, p_rs,
    ct_ss, ct_rs, st_ss, st_rs, gr_ss, gr_rs, hy_ss, hy_rs,
    d_ss, d_rs, m1_ss, m1_rs, m2_ss, m2_rs, y_ss, y_rs,
):
    z, h, x = lax.axis_index("z"), lax.axis_index("h"), lax.axis_index("x")
    ell, core = lax.axis_index("l"), lax.axis_index("c")
    me = z * H + h
    z_up, z_down = lax.rem(z + 1, Z), lax.rem(z + Z - 1, Z)
    x_up, x_down, x_far = lax.rem(x + 1, X), lax.rem(x + X - 1, X), lax.rem(x + 2, X)
    sends = []

    coef_own[...] = jnp.zeros_like(coef_own)
    coef_own[:, 0:M] = res[0]
    coef_own[:, M:2 * M] = rate[0]
    local = [
        pltpu.make_async_copy(tok, tk.at[rows_of(x, POS), :], loc_sem.at[0]),
        pltpu.make_async_copy(wts, wg.at[:, rows_of(me, OWN), :], loc_sem.at[1]),
        pltpu.make_async_copy(cot.at[:, x], cotv.at[x], loc_sem.at[2]),
    ]
    for copy in local:
        copy.start()
    coef[rows_of(me, OWN), :] = coef_own[...]

    barrier = pltpu.get_barrier_semaphore()
    peers = [{"z": z_up}, {"z": z_down}, {"h": 1 - h}, {"c": 1 - core}]
    peers += [{"x": lax.rem(x + i, X)} for i in range(1, X)]
    peers += [{"l": lax.rem(ell + i, NL)} for i in range(1, NL)]
    for peer in peers:
        pl.semaphore_signal(barrier, inc=1, device_id=peer, device_id_type=MESH)
    pl.semaphore_wait(barrier, len(peers))

    def launch(copies):
        for copy in copies:
            copy.start()
            sends.append(copy)
        return copies

    def arrived(copies):
        for copy in copies:
            copy.wait_recv()

    def ring(stream, way, step, p):
        from_z = lax.rem(z - step + Z, Z) if way == 0 else lax.rem(z + step, Z)
        block = from_z * H + (h if stream == 0 else 1 - h)
        cut = pl.ds(p % 2 * CUT, CUT)
        slot = wg.at[p // 2, rows_of(block, OWN), cut]
        own = stream == 0 and step == 0
        to = {"z": z_up if way == 0 else z_down}
        at = (stream, way, step)
        copies = [remote(wts.at[p // 2, :, cut] if own else slot, slot, w_ss.at[at + (p,)], w_rs.at[at + (p,)], to)]
        if p == 0:
            slot = coef.at[rows_of(block, OWN), :]
            copies.append(remote(coef_own if own else slot, slot, c_ss.at[at], c_rs.at[at], to))
        return copies

    def unit(source, u):
        return tk.at[pl.ds(pl.multiple_of(source * POS + core * (POS // 2) + u * UNIT, UNIT), UNIT), :]

    def near(way, u):
        src = tok.at[pl.ds(pl.multiple_of(core * (POS // 2) + u * UNIT, UNIT), UNIT), :]
        to = {"x": x_up if way == 0 else x_down}
        return [remote(src, unit(x, u), t_ss.at[way, u], t_rs.at[way, u], to)]

    def far(way):
        to = {"x": x_up if way == 0 else x_down}
        src = unit(x_down if way == 0 else x_up, way)
        return [remote(src, src, t_ss.at[way, 2], t_rs.at[way, 2], to)]

    def pass_on(index, source, u):
        src = unit(source, u)
        return [remote(src, src, p_ss.at[index], p_rs.at[index], {"c": 1 - core})]

    def to_mate(p):
        cut = pl.ds(p % 2 * CUT, CUT)
        copies = [remote(
            wts.at[p // 2, :, cut], wg.at[p // 2, rows_of(me, OWN), cut], h_ss.at[p], h_rs.at[p], {"h": 1 - h}
        )]
        if p == 0:
            copies.append(remote(coef_own, coef.at[rows_of(me, OWN), :], h_ss.at[CHUNKS], h_rs.at[CHUNKS], {"h": 1 - h}))
        return copies

    flying = {}
    for p in range(CHUNKS):
        for way in (0, 1):
            flying["ring", 0, way, 0, p] = launch(ring(0, way, 0, p))
        flying["mate", p] = launch(to_mate(p))
    for way, u in ((0, 0), (1, 1), (0, 1), (1, 0)):
        flying["near", way, u] = launch(near(way, u))
    cots = launch([
        remote(cot.at[:, lax.rem(x + i, X)], cotv.at[x], ct_ss.at[i - 1], ct_rs.at[i - 1], {"x": lax.rem(x + i, X)})
        for i in range(1, X)
    ])
    def turn_cotangent(i, carry):
        cot_s[rows_of(i, POS), :] = jnp.transpose(cotv[i].astype(F32).reshape(CH, POS))
        return carry

    order = arrival_order()
    last_coef = max(i for i, message in enumerate(order) if message[0] == "ring" and message[4] == 0)
    for i, message in enumerate(order):
        arrived(flying[message])
        if message[0] == "ring":
            _, stream, way, step, p = message
            if step + 1 < STEPS[stream][way]:
                flying["ring", stream, way, step + 1, p] = launch(ring(stream, way, step + 1, p))
        elif message[0] == "mate":
            for way in (0, 1):
                flying["ring", 1, way, 0, message[1]] = launch(ring(1, way, 0, message[1]))
        elif message[0] == "near":
            _, way, u = message
            if u == way:
                flying["far", way] = launch(far(way))
            flying["pass", 2 * way + u] = launch(pass_on(2 * way + u, x_down if way == 0 else x_up, u))
        elif message[0] == "far":
            way = message[1]
            flying["pass", 4 + way] = launch(pass_on(4 + way, x_far, way))
        if i == len(order) * 2 // 3:
            arrived(cots)
            for copy in local:
                copy.wait()
            lax.fori_loop(0, X, turn_cotangent, 0)
        if i == last_coef:
            by_mode = jnp.transpose(coef[...])
            residue, decay = by_mode[0:M, :], by_mode[M:2 * M, :]
            width = jnp.sqrt(2.0 * decay)
            once, scaled = jnp.exp(-decay), residue * width
            for m in range(M):
                a_t[m] = jnp.broadcast_to(once[m:m + 1, :], (8, CH))
                r_t[m] = jnp.broadcast_to(scaled[m:m + 1, :], (8, CH))

    def project(i, carry):
        out = lax.dot_general(
            tk[rows_of(i, POS), :], wg[...].reshape(3 * CH, D),
            (((1,), (1,)), ((), ())), preferred_element_type=F32,
        )
        q_s[rows_of(i, POS), :] = rounded(out[:, 0:CH])
        k_s[rows_of(i, POS), :] = rounded(out[:, CH:2 * CH])
        v_s[rows_of(i, POS), :] = rounded(out[:, 2 * CH:3 * CH])
        return carry

    lax.fori_loop(0, X, project, 0)

    def gate(i, carry):
        at = rows_of(i, POS)
        g_s[at, :] = rounded(k_s[at, :] * v_s[at, :])
        s_s[at, :] = rounded(cot_s[at, :] * q_s[at, :])
        return carry

    lax.fori_loop(0, X, gate, 0)

    def states(t, carry):
        up, down = carry
        g_now = g_s[pl.ds(t, 8, stride=SUB), :]
        s_now = s_s[pl.ds(SUB - 1 - t, 8, stride=SUB), :]
        return (
            tuple(a_t[m] * up[m] + g_now for m in range(M)),
            tuple(a_t[m] * down[m] + s_now for m in range(M)),
        )

    zero = tuple(jnp.zeros((8, CH), F32) for _ in range(M))
    up, down = lax.fori_loop(0, SUB, states, (zero, zero))
    piece = lax.broadcasted_iota(jnp.int32, (8, CH), 0)
    for m in range(M):
        lost = decay[m:m + 1, :]
        fore, aft = up[m], down[m]
        for shift in (1, 2, 4):
            keep = jnp.exp(lost * (-float(SUB * shift)))
            fore = fore + jnp.where(piece >= shift, keep * pltpu.roll(fore, shift, 0), 0.0)
            aft = aft + jnp.where(piece < 8 - shift, keep * pltpu.roll(aft, 8 - shift, 0), 0.0)
        eb[0, m:m + 1, :] = fore[7:8, :]
        eb[1, m:m + 1, :] = aft[0:1, :]
        cl_t[m] = jnp.where(piece >= 1, pltpu.roll(fore, 1, 0), 0.0)
        cb_t[m] = jnp.where(piece < 7, pltpu.roll(aft, 7, 0), 0.0)

    states_out = []
    for i in sorted(range(1, ZH), key=lambda i: (-(i % H), abs(i - ZH // 2))):
        to = lax.rem(me + i, ZH)
        which = jnp.where(to > me, 0, 1)
        states_out.append(remote(
            eb.at[which], st.at[me], st_ss.at[i], st_rs.at[i],
            {"z": lax.div(to, H), "h": lax.rem(to, H)},
        ))
    launch(states_out)
    arrived(states_out)

    far_keep = jnp.exp(decay * (-float(ROWS)))
    none = jnp.zeros((M, CH), F32)
    before = lax.fori_loop(0, me, lambda j, s: far_keep * s + st[j], none)
    after = lax.fori_loop(0, ZH - 1 - me, lambda j, s: far_keep * s + st[ZH - 1 - j], none)

    place = piece.astype(F32) * float(SUB)
    start_up, start_down = [], []
    for m in range(M):
        lost = decay[m:m + 1, :]
        start_up.append(cl_t[m] + jnp.exp(-lost * place) * before[m:m + 1, :])
        start_down.append(
            cb_t[m] + jnp.exp(-lost * (float(SUB * 7) - place)) * after[m:m + 1, :]
        )

    def forward(t, carry):
        up, total = carry
        at = pl.ds(t, 8, stride=SUB)
        g_now, s_now = g_s[at, :], s_s[at, :]
        up = tuple(a_t[m] * up[m] + g_now for m in range(M))
        conv_s[at, :] = tree_sum(r_t[m] * up[m] for m in range(M))
        return up, tuple(total[m] + s_now * up[m] for m in range(M))

    def backward(t, down):
        at = pl.ds(SUB - 1 - t, 8, stride=SUB)
        s_now = s_s[at, :]
        down = tuple(a_t[m] * down[m] + s_now for m in range(M))
        back_s[at, :] = tree_sum(r_t[m] * down[m] for m in range(M))
        return down

    _, total = lax.fori_loop(0, SUB, forward, (tuple(start_up), zero))
    lax.fori_loop(0, SUB, backward, tuple(start_down))

    def gates(i, carry):
        at = rows_of(i, POS)
        conv, back = rounded(conv_s[at, :]), rounded(back_s[at, :])
        g_mat[at, 0:CH] = (cot_s[at, :] * conv).astype(BF16)
        g_mat[at, CH:2 * CH] = (back * v_s[at, :]).astype(BF16)
        g_mat[at, 2 * CH:3 * CH] = (back * k_s[at, :]).astype(BF16)
        return carry

    lax.fori_loop(0, X, gates, 0)

    def outputs(i, carry):
        at = rows_of(i, POS)
        hyena = jnp.transpose(q_s[at, :] * rounded(conv_s[at, :]))
        hy_t[i] = hyena.reshape(ZH, OWN, POS).astype(BF16)
        return carry

    def send_outputs():
        lax.fori_loop(0, X, outputs, 0)
        hyenas = launch([
            remote(
                hy_t.at[lax.rem(x + i, X)], hy_o.at[:, x], hy_ss.at[i - 1], hy_rs.at[i - 1],
                {"x": lax.rem(x + i, X)},
            )
            for i in range(1, X)
        ])
        hy_o[:, x] = hy_t[x]
        gr_s[...] = jnp.zeros_like(gr_s)
        norm = 1.0 / math.sqrt(length)
        for m in range(M):
            gr_s[m:m + 1, :] = jnp.sum(total[m], axis=0, keepdims=True) * (width[m:m + 1, :] * norm)
        gr_t[...] = jnp.transpose(gr_s[...])
        owners = []
        for i in range(1, ZH):
            to = lax.rem(me + i, ZH)
            owners.append(remote(
                gr_t.at[rows_of(to, OWN), :], gr_r.at[i], gr_ss.at[i], gr_rs.at[i],
                {"z": lax.div(to, H), "h": lax.rem(to, H)},
            ))
        return hyenas, launch(owners)

    def product(j, mine):
        parity = core if mine else 1 - core
        col = pl.multiple_of((j // PARTS * NC + parity) * COLS + j % PARTS * WIDE, WIDE)

        def tile(i, carry):
            at = rows_of(i, 2 * POS)
            out = jnp.dot(
                g_mat[at, :], wg[:, :, pl.ds(col, WIDE)].reshape(3 * CH, WIDE),
                preferred_element_type=F32,
            )
            if mine:
                acc[j, at, :] = out
            else:
                d_s[j, at, :] = out.astype(BF16)
            return carry

        lax.fori_loop(0, ROWS // (2 * POS), tile, 0)

    def chip_sum(j, owner):
        at = rows_of(owner, POS)
        return acc[j, at, :] + d_r[j, at, :].astype(F32)

    cores, first, second, finals = {}, {}, {}, {}

    def stage_product(j):
        product(j, False)
        cores[j] = launch((remote(d_s.at[j], d_r.at[j], d_ss.at[j], d_rs.at[j], {"c": 1 - core}),))
        product(j, True)

    def stage_first(j):
        arrived(cores[j])
        other = chip_sum(j, x_far)
        m1_s[j, 0] = other[:, 0:HALF].astype(BF16)
        m1_s[j, 1] = other[:, HALF:WIDE].astype(BF16)
        first[j] = launch([
            remote(m1_s.at[j, w], m1_r.at[j, w], m1_ss.at[j, w], m1_rs.at[j, w], {"x": x_up if w == 0 else x_down})
            for w in (0, 1)
        ])

    def stage_second(j):
        arrived(first[j])
        for w in (0, 1):
            side = chip_sum(j, x_up if w == 0 else x_down)
            cut = slice(0, HALF) if w == 0 else slice(HALF, WIDE)
            rest = slice(HALF, WIDE) if w == 0 else slice(0, HALF)
            m2_s[j, w, :, cut] = (side[:, cut] + m1_r[j, w].astype(F32)).astype(BF16)
            m2_s[j, w, :, rest] = side[:, rest].astype(BF16)
        second[j] = launch([
            remote(m2_s.at[j, w], m2_r.at[j, w], m2_ss.at[j, w], m2_rs.at[j, w], {"x": x_up if w == 0 else x_down})
            for w in (0, 1)
        ])

    def stage_third(j):
        arrived(second[j])
        total_x = chip_sum(j, x) + m2_r[j, 0].astype(F32) + m2_r[j, 1].astype(F32)
        owner, part = j // PARTS, j % PARTS
        copy = remote(
            y_s.at[j], y_r.at[ell, part], y_ss.at[j], y_rs.at[ell, part], {"l": jnp.int32(owner)}
        )
        finals[j] = copy

        @pl.when(ell == owner)
        def _():
            y_own[part] = total_x

        @pl.when(ell != owner)
        def _():
            y_s[j] = total_x.astype(BF16)
            copy.start()

    for i in range(PIECES + 7):
        for late, stage in ((0, stage_product), (2, stage_first), (5, stage_second), (7, stage_third)):
            if 0 <= i - late < PIECES:
                stage(ORDER[i - late])
        if i == 1:
            hyenas, owners = send_outputs()

    arrived(hyenas)
    hyena_out[...] = hy_o[...]
    arrived(owners)
    share = gr_t[rows_of(me, OWN), :]
    for i in range(1, ZH):
        share = share + gr_r[i]
    grad_residue[...] = share[:, 0:M]
    for j in range(NL):
        @pl.when(ell != j)
        def _():
            for part in range(PARTS):
                piece_at = j * PARTS + part
                remote(
                    y_s.at[piece_at], y_r.at[j, part], y_ss.at[piece_at], y_rs.at[j, part], {"l": jnp.int32(j)}
                ).wait_recv()
                y_own[part] += y_r[j, part].astype(F32)
                finals[piece_at].wait_send()
    for part in range(PARTS):
        grad_input[:, part * WIDE:(part + 1) * WIDE] = y_own[part].astype(BF16)
    for copy in sends:
        copy.wait_send()


def shards(tokens, weights, residues, decay_rates, cotangent, length):
    wts = jnp.transpose(weights[0], (1, 0, 2))
    cot = cotangent.reshape(ZH, X, OWN, POS)
    dma = pltpu.SemaphoreType.DMA
    scratch = [
        pltpu.VMEM((ROWS, D), BF16),
        pltpu.VMEM((3, CH, D), BF16),
        pltpu.VMEM((OWN, 128), F32),
        pltpu.VMEM((CH, 128), F32),
        pltpu.VMEM((X, ZH, OWN, POS), BF16),
    ]
    scratch += [pltpu.VMEM((ROWS, CH), F32)] * 8
    scratch += [pltpu.VMEM((M, 8, CH), F32)] * 4
    scratch += [
        pltpu.VMEM((2, M, CH), F32),
        pltpu.VMEM((ZH, M, CH), F32),
        pltpu.VMEM((CH, CH), F32),
        pltpu.VMEM((CH, CH), F32),
        pltpu.VMEM((ZH, OWN, CH), F32),
        pltpu.VMEM((X, ZH, OWN, POS), BF16),
        pltpu.VMEM((ZH, X, OWN, POS), BF16),
        pltpu.VMEM((ROWS, 3 * CH), BF16),
        pltpu.VMEM((PIECES, ROWS, WIDE), F32),
        pltpu.VMEM((PIECES, ROWS, WIDE), BF16),
        pltpu.VMEM((PIECES, ROWS, WIDE), BF16),
        pltpu.VMEM((PIECES, 2, POS, HALF), BF16),
        pltpu.VMEM((PIECES, 2, POS, HALF), BF16),
        pltpu.VMEM((PIECES, 2, POS, WIDE), BF16),
        pltpu.VMEM((PIECES, 2, POS, WIDE), BF16),
        pltpu.VMEM((PIECES, POS, WIDE), BF16),
        pltpu.VMEM((NL, PARTS, POS, WIDE), BF16),
        pltpu.VMEM((PARTS, POS, WIDE), F32),
    ]
    steps = Z // 2
    scratch += [dma((3,))]
    for shape in (
        (2, 2, steps, CHUNKS), (2, 2, steps), (CHUNKS + 1,), (2, 3), (6,), (X - 1,), (ZH,), (ZH,), (X - 1,),
        (PIECES,), (PIECES, 2), (PIECES, 2),
    ):
        scratch += [dma(shape), dma(shape)]
    scratch += [dma((PIECES,)), dma((NL, PARTS))]
    vmem, hbm = pl.BlockSpec(memory_space=pltpu.VMEM), pl.BlockSpec(memory_space=pl.ANY)
    hyena, grad, residue = pl.pallas_call(
        functools.partial(body, length),
        out_shape=(
            jax.ShapeDtypeStruct((ZH, X, OWN, POS), BF16),
            jax.ShapeDtypeStruct((POS, COLS), BF16),
            jax.ShapeDtypeStruct((OWN, M), F32),
        ),
        in_specs=[hbm, hbm, vmem, vmem, hbm],
        out_specs=(vmem, vmem, vmem),
        scratch_shapes=scratch,
        compiler_params=pltpu.CompilerParams(
            collective_id=0, has_side_effects=True, vmem_limit_bytes=60 * 1024 * 1024
        ),
        name="hyena_block",
    )(tokens, wts, residues, decay_rates, cot)
    return (hyena.reshape(X * ZH * OWN, POS), grad, residue[None])


def solution(mesh):
    fine = Mesh(mesh.devices.reshape(SIZES), AXES)
    ctx, tp = ("z", "h", "x"), ("l", "c")

    def step(tokens, weights, residues, decay_rates, cotangent):
        return jax.shard_map(
            functools.partial(shards, length=tokens.shape[0]),
            mesh=fine,
            in_specs=(P(ctx, None), P(tp, ctx), P(tp, ctx), P(tp, ctx), P(tp, ctx)),
            out_specs=(P(tp, ctx), P(ctx, tp), P(tp, ctx)),
            check_vma=False,
        )(tokens, weights, residues, decay_rates, cotangent)

    return step
```

time: 112 us -> 101 us (0.902)
  Pallas kernels: 108 us -> 97.1 us
    pallas_call x1, Pallas kernels: 108 us -> 97.1 us  [shards(): pl.pallas_call(functools.partial(body, length), out_shape=(jax.ShapeDtype...]
where the time goes in v1:
time: 101 us
  Pallas kernels  97.1 us (96%)
  local copies, waits for them, and re-layouts  2.88 us (3%)
    pallas_call x1, Pallas kernels, shards(): pl.pallas_call(functools.partial(body, length), out_shape=(jax.ShapeDtype...  97.1 us
    unnamed x7, local copies, waits for them, and re-layouts  2.88 us

profile of v1, /device:TPU:16, one launch (start us, length us, event | category | flops | bytes accessed | tf_op | source)
XLA Modules:
  0.0 100.6 jit_solution(3421132066846612934)
XLA Ops:
  0.6 97.1 %hyena_block.1 = (bf16[16,4,8,128]{3,2,1,0:T(8,128)(2,1)}, bf16[128,512]{1,0:T(8,128)(2,1)}, f32[8,16]{1,0:T(8,128)}) custom-call(bf16[128,4096]{1,0:T(8,128)(2,1)} %tok.1, bf16[3,8,4096]{2,1,0:T(8,128)(2,1)} %bitcast.6, f32[1,8,16]{2,1,0:T(8,128)} %res.1, f32[1,8,16]{2,1,0:T(8,128)} %rate.1, bf16[16,4,8,128]{3,2,1,0:T(8,128)(2,1)} %bitcast.8), custom_call_target="tpu_custom_call" | custom-call | tf_op jit(solution)/shard_map/hyena_block/pallas_call | solution.py:506
  97.7 0.0 copy-start
  97.7 1.6 %copy.11 = bf16[512,128]{1,0:T(8,128)(2,1)} copy(bf16[512,128]{1,0:T(8,128)(2,1)} %bitcast.7) | data formatting | bytes 262144
  99.3 0.0 copy-done
  99.3 0.0 copy-start.1
  99.3 0.7 copy.12
  100.0 0.0 copy-done.1
  100.0 0.6 copy.13
Async XLA Ops:
  97.7 1.6 %copy-start = (bf16[128,512]{1,0:T(8,128)(2,1)S(1)}, bf16[128,512]{1,0:T(8,128)(2,1)}, u32[]{:S(2)}) copy-start(bf16[128,512]{1,0:T(8,128)(2,1)} %get-tuple-element.13) | copy-start | bytes 393220
  99.3 0.7 copy-start.1

commit v2 on v1

--- a/solution.py
+++ b/solution.py
@@ -459,6 +459,12 @@
         grad_input[:, part * WIDE:(part + 1) * WIDE] = y_own[part].astype(BF16)
     for copy in sends:
         copy.wait_send()
+
+
+def hand_over(hyena, grad, residue, hyena_out, grad_out, residue_out):
+    hyena_out[...] = hyena[...]
+    grad_out[...] = grad[...]
+    residue_out[...] = residue[...]
 
 
 def shards(tokens, weights, residues, decay_rates, cotangent, length):
@@ -506,9 +512,9 @@
     hyena, grad, residue = pl.pallas_call(
         functools.partial(body, length),
         out_shape=(
-            jax.ShapeDtypeStruct((ZH, X, OWN, POS), BF16),
-            jax.ShapeDtypeStruct((POS, COLS), BF16),
-            jax.ShapeDtypeStruct((OWN, M), F32),
+            pltpu.VMEM((ZH, X, OWN, POS), BF16),
+            pltpu.VMEM((POS, COLS), BF16),
+            pltpu.VMEM((OWN, M), F32),
         ),
         in_specs=[hbm, hbm, vmem, vmem, hbm],
         out_specs=(vmem, vmem, vmem),
@@ -518,6 +524,18 @@
         ),
         name="hyena_block",
     )(tokens, wts, residues, decay_rates, cot)
+    hyena, grad, residue = pl.pallas_call(
+        hand_over,
+        out_shape=(
+            jax.ShapeDtypeStruct((ZH, X, OWN, POS), BF16),
+            jax.ShapeDtypeStruct((POS, COLS), BF16),
+            jax.ShapeDtypeStruct((OWN, M), F32),
+        ),
+        in_specs=[vmem, vmem, vmem],
+        out_specs=(vmem, vmem, vmem),
+        compiler_params=pltpu.CompilerParams(vmem_limit_bytes=4 * 1024 * 1024),
+        name="results",
+    )(hyena, grad, residue)
     return (hyena.reshape(X * ZH * OWN, POS), grad, residue[None])
 
 

time: 101 us -> 97.9 us (0.969)
  local copies, waits for them, and re-layouts: 2.88 us -> 0 us
    unnamed x7 -> x0, local copies, waits for them, and re-layouts: 2.88 us -> none
    pallas_call x1 -> x2, Pallas kernels: 97.1 us -> 97.1 us  [the longest x1 96.4 us: shards(): pl.pallas_call(functools.partial(body, length), out_shape=(pltpu.VMEM((ZH...]
where the time goes in v2:
time: 97.9 us; the launch traced here: 97.8 us
  Pallas kernels  97.1 us (99%)
    pallas_call x1, Pallas kernels, shards(): pl.pallas_call(functools.partial(body, length), out_shape=(pltpu.VMEM((ZH...  96.4 us

profile of v2, /device:TPU:16, one launch (start us, length us, event | category | flops | bytes accessed | tf_op | source)
XLA Modules:
  0.0 97.8 jit_solution(6176148330886866862)
XLA Ops:
  0.6 96.4 %hyena_block.1 = (bf16[16,4,8,128]{3,2,1,0:T(8,128)(2,1)S(1)}, bf16[128,512]{1,0:T(8,128)(2,1)S(1)}, f32[8,16]{1,0:T(8,128)S(1)}) custom-call(bf16[128,4096]{1,0:T(8,128)(2,1)} %tok.1, bf16[3,8,4096]{2,1,0:T(8,128)(2,1)} %bitcast.6, f32[1,8,16]{2,1,0:T(8,128)} %res.1, f32[1,8,16]{2,1,0:T(8,128)} %rate.1, bf16[16,4,8,128]{3,2,1,0:T(8,128)(2,1)} %bitcast.7), custom_call_target="tpu_custom_call" | custom-call | tf_op jit(solution)/shard_map/hyena_block/pallas_call | solution.py:512
  97.0 0.7 results.1

commit v3 on v2

--- a/solution.py
+++ b/solution.py
@@ -236,15 +236,15 @@
 
     def project(i, carry):
         out = lax.dot_general(
-            tk[rows_of(i, POS), :], wg[...].reshape(3 * CH, D),
+            tk[rows_of(i, ROWS // 2), :], wg[...].reshape(3 * CH, D),
             (((1,), (1,)), ((), ())), preferred_element_type=F32,
         )
-        q_s[rows_of(i, POS), :] = rounded(out[:, 0:CH])
-        k_s[rows_of(i, POS), :] = rounded(out[:, CH:2 * CH])
-        v_s[rows_of(i, POS), :] = rounded(out[:, 2 * CH:3 * CH])
+        q_s[rows_of(i, ROWS // 2), :] = rounded(out[:, 0:CH])
+        k_s[rows_of(i, ROWS // 2), :] = rounded(out[:, CH:2 * CH])
+        v_s[rows_of(i, ROWS // 2), :] = rounded(out[:, 2 * CH:3 * CH])
         return carry
 
-    lax.fori_loop(0, X, project, 0)
+    lax.fori_loop(0, 2, project, 0)
 
     def gate(i, carry):
         at = rows_of(i, POS)
@@ -366,7 +366,7 @@
         col = pl.multiple_of((j // PARTS * NC + parity) * COLS + j % PARTS * WIDE, WIDE)
 
         def tile(i, carry):
-            at = rows_of(i, 2 * POS)
+            at = rows_of(i, ROWS)
             out = jnp.dot(
                 g_mat[at, :], wg[:, :, pl.ds(col, WIDE)].reshape(3 * CH, WIDE),
                 preferred_element_type=F32,
@@ -377,7 +377,7 @@
                 d_s[j, at, :] = out.astype(BF16)
             return carry
 
-        lax.fori_loop(0, ROWS // (2 * POS), tile, 0)
+        tile(0, 0)
 
     def chip_sum(j, owner):
         at = rows_of(owner, POS)

time: 97.9 us -> 95.4 us (0.974)
  Pallas kernels: 97.1 us -> 94.6 us
    pallas_call x1, Pallas kernels: 96.4 us -> 93.9 us  [shards(): pl.pallas_call(functools.partial(body, length), out_shape=(pltpu.VMEM((ZH...]
where the time goes in v3:
time: 95.4 us; the launch traced here: 95.2 us
  Pallas kernels  94.6 us (99%)
    pallas_call x1, Pallas kernels, shards(): pl.pallas_call(functools.partial(body, length), out_shape=(pltpu.VMEM((ZH...  93.9 us

profile of v3, /device:TPU:16, one launch (start us, length us, event | category | flops | bytes accessed | tf_op | source)
XLA Modules:
  0.0 95.2 jit_solution(12318345137787865062)
XLA Ops:
  0.6 93.9 %hyena_block.1 = (bf16[16,4,8,128]{3,2,1,0:T(8,128)(2,1)S(1)}, bf16[128,512]{1,0:T(8,128)(2,1)S(1)}, f32[8,16]{1,0:T(8,128)S(1)}) custom-call(bf16[128,4096]{1,0:T(8,128)(2,1)} %tok.1, bf16[3,8,4096]{2,1,0:T(8,128)(2,1)} %bitcast.6, f32[1,8,16]{2,1,0:T(8,128)} %res.1, f32[1,8,16]{2,1,0:T(8,128)} %rate.1, bf16[16,4,8,128]{3,2,1,0:T(8,128)(2,1)} %bitcast.7), custom_call_target="tpu_custom_call" | custom-call | tf_op jit(solution)/shard_map/hyena_block/pallas_call | solution.py:512
  94.5 0.7 results.1

commit v4 on v3

--- a/solution.py
+++ b/solution.py
@@ -116,6 +116,13 @@
     x_up, x_down, x_far = lax.rem(x + 1, X), lax.rem(x + X - 1, X), lax.rem(x + 2, X)
     sends = []
 
+    barrier = pltpu.get_barrier_semaphore()
+    peers = [{"z": z_up}, {"z": z_down}, {"h": 1 - h}, {"c": 1 - core}]
+    peers += [{"x": lax.rem(x + i, X)} for i in range(1, X)]
+    peers += [{"l": lax.rem(ell + i, NL)} for i in range(1, NL)]
+    for peer in peers:
+        pl.semaphore_signal(barrier, inc=1, device_id=peer, device_id_type=MESH)
+
     coef_own[...] = jnp.zeros_like(coef_own)
     coef_own[:, 0:M] = res[0]
     coef_own[:, M:2 * M] = rate[0]
@@ -127,13 +134,6 @@
     for copy in local:
         copy.start()
     coef[rows_of(me, OWN), :] = coef_own[...]
-
-    barrier = pltpu.get_barrier_semaphore()
-    peers = [{"z": z_up}, {"z": z_down}, {"h": 1 - h}, {"c": 1 - core}]
-    peers += [{"x": lax.rem(x + i, X)} for i in range(1, X)]
-    peers += [{"l": lax.rem(ell + i, NL)} for i in range(1, NL)]
-    for peer in peers:
-        pl.semaphore_signal(barrier, inc=1, device_id=peer, device_id_type=MESH)
     pl.semaphore_wait(barrier, len(peers))
 
     def launch(copies):
@@ -286,7 +286,11 @@
             eb.at[which], st.at[me], st_ss.at[i], st_rs.at[i],
             {"z": lax.div(to, H), "h": lax.rem(to, H)},
         ))
+    gathered = list(sends)
+    sends.clear()
     launch(states_out)
+    for copy in gathered:
+        copy.wait_send()
     arrived(states_out)
 
     far_keep = jnp.exp(decay * (-float(ROWS)))
@@ -437,14 +441,15 @@
                 stage(ORDER[i - late])
         if i == 1:
             hyenas, owners = send_outputs()
-
-    arrived(hyenas)
-    hyena_out[...] = hy_o[...]
-    arrived(owners)
-    share = gr_t[rows_of(me, OWN), :]
-    for i in range(1, ZH):
-        share = share + gr_r[i]
-    grad_residue[...] = share[:, 0:M]
+        if i == PIECES + 3:
+            arrived(hyenas)
+            hyena_out[...] = hy_o[...]
+            arrived(owners)
+            share = gr_t[rows_of(me, OWN), :]
+            for source in range(1, ZH):
+                share = share + gr_r[source]
+            grad_residue[...] = share[:, 0:M]
+
     for j in range(NL):
         @pl.when(ell != j)
         def _():

time: 95.4 us -> 95.2 us (level)
  no operation moved by 1% of the time
where the time goes in v4:
time: 95.2 us; the launch traced here: 95 us
  Pallas kernels  94.4 us (99%)
    pallas_call x1, Pallas kernels, shards(): pl.pallas_call(functools.partial(body, length), out_shape=(pltpu.VMEM((ZH...  93.7 us

profile of v4, /device:TPU:16, one launch (start us, length us, event | category | flops | bytes accessed | tf_op | source)
XLA Modules:
  0.0 95.0 jit_solution(14394162032697022628)
XLA Ops:
  0.6 93.7 %hyena_block.1 = (bf16[16,4,8,128]{3,2,1,0:T(8,128)(2,1)S(1)}, bf16[128,512]{1,0:T(8,128)(2,1)S(1)}, f32[8,16]{1,0:T(8,128)S(1)}) custom-call(bf16[128,4096]{1,0:T(8,128)(2,1)} %tok.1, bf16[3,8,4096]{2,1,0:T(8,128)(2,1)} %bitcast.6, f32[1,8,16]{2,1,0:T(8,128)} %res.1, f32[1,8,16]{2,1,0:T(8,128)} %rate.1, bf16[16,4,8,128]{3,2,1,0:T(8,128)(2,1)} %bitcast.7), custom_call_target="tpu_custom_call" | custom-call | tf_op jit(solution)/shard_map/hyena_block/pallas_call | solution.py:517
  94.3 0.7 results.1
